TPU v7x, 128 devices: a whole 4x4x4 slice. The times are simulated.
128 devices in a mesh: node: 8 (over z, core), event: 16 (over x, y).
Axes of the slice: x: 4, y: 4, z: 4, core: 2. Of those that a mesh axis runs over, the one named last changes fastest.
Arguments:
- memory: bfloat16 [16384, 256], P('node'), may hold values from -6 to 6
- event_feat: bfloat16 [128, 128, 16, 128], P(('node', 'event')), may hold values from -6 to 6
- event_source: int32 [128, 128, 16], P(('node', 'event')), may hold values from 0 to 2047
- event_partner: int32 [128, 128, 16], P(('node', 'event')), may hold values from 0 to 1023
- event_negative: int32 [128, 128, 16], P(('node', 'event')), may hold values from 0 to 1023
- event_time: int32 [128, 128, 16], P(('node', 'event')), may hold values from 0 to 1023
- event_count: int32 [128, 128], P(('node', 'event')), may hold values from 0 to 16, as said below
- requests: int32 [128, 8, 128], P(('node', 'event')), may hold values from 0 to 2047
- w_input: bfloat16 [512, 768], replicated, may hold values from -0.25 to 0.25
- w_state: bfloat16 [256, 768], replicated, may hold values from -0.375 to 0.375
- w_pair: bfloat16 [256, 256], replicated, may hold values from -0.375 to 0.375
- gate_bias: float32 [768], replicated, may hold values from -3 to 3
- time_freq: float32 [128], replicated, may hold values from 0.001 to 1
Outputs:
- memory_grad: float32 [16384, 256], P(('node', 'event'))
Inputs may be any that keep to these rules, and one draw needn't show every extreme that they name: `event_count`: in every draw some device receives 16 live slots from every time block.
All inputs are finite; a program needn't handle non-finite values.
Results may differ from a plain program's by a relative error of at most 0.0021.
Values may be sent and summed in bfloat16 or wider, within the bound.
No kernel may reach another device: no remote copies, remote signals or barrier semaphores. Data moves between devices by JAX's collectives and lax.ppermute only.
A program may use at most 64 MiB of HBM per device.

v0:
```python
import math

import jax
import jax.numpy as jnp
from jax import lax
from jax.sharding import PartitionSpec as P


def pair_grads(
    current, partner, negative, feature, timing, valid, w_input, w_state, w_pair, gate_bias
):
    width = current.shape[1]
    joined = jnp.concatenate([partner, feature, timing], axis=1)
    from_input = jnp.dot(joined, w_input, preferred_element_type=jnp.float32)
    from_state = jnp.dot(current, w_state, preferred_element_type=jnp.float32)
    reset = jax.nn.sigmoid(from_input[:, :width] + from_state[:, :width] + gate_bias[:width])
    update = jax.nn.sigmoid(
        from_input[:, width : 2 * width]
        + from_state[:, width : 2 * width]
        + gate_bias[width : 2 * width]
    )
    recurrent = from_state[:, 2 * width :]
    candidate = jnp.tanh(from_input[:, 2 * width :] + gate_bias[2 * width :] + reset * recurrent)
    previous = current.astype(jnp.float32)
    renewed = (1.0 - update) * candidate + update * previous
    factor = 1.0 / math.sqrt(width)
    key_pos = jnp.dot(partner, w_pair, preferred_element_type=jnp.float32)
    key_neg = jnp.dot(negative, w_pair, preferred_element_type=jnp.float32)
    score_pos = jnp.sum(renewed * key_pos, axis=1) * factor
    score_neg = jnp.sum(renewed * key_neg, axis=1) * factor
    weight_pos = -valid * jax.nn.sigmoid(-score_pos)
    weight_neg = valid * jax.nn.sigmoid(score_neg)
    grad_renewed = (weight_pos[:, None] * key_pos + weight_neg[:, None] * key_neg) * factor
    grad_keypos = (weight_pos[:, None] * renewed * factor).astype(jnp.bfloat16)
    grad_keyneg = (weight_neg[:, None] * renewed * factor).astype(jnp.bfloat16)
    grad_cand = grad_renewed * (1.0 - update) * (1.0 - candidate * candidate)
    grad_reset = grad_cand * recurrent * reset * (1.0 - reset)
    grad_update = grad_renewed * (previous - candidate) * update * (1.0 - update)
    input_back = jnp.concatenate([grad_reset, grad_update, grad_cand], axis=1).astype(jnp.bfloat16)
    state_back = jnp.concatenate([grad_reset, grad_update, grad_cand * reset], axis=1).astype(
        jnp.bfloat16
    )
    through_input = jnp.dot(input_back, w_input.T, preferred_element_type=jnp.float32)
    grad_current = grad_renewed * update + jnp.dot(
        state_back, w_state.T, preferred_element_type=jnp.float32
    )
    grad_partner = through_input[:, :width] + jnp.dot(
        grad_keypos, w_pair.T, preferred_element_type=jnp.float32
    )
    grad_negative = jnp.dot(grad_keyneg, w_pair.T, preferred_element_type=jnp.float32)
    return (grad_current, grad_partner, grad_negative)


def pick_rows(values, row_ids):
    selector = (row_ids[:, None] == jnp.arange(values.shape[0], dtype=jnp.int32)[None, :]).astype(
        values.dtype
    )
    return jnp.dot(selector, values, preferred_element_type=jnp.float32).astype(values.dtype)


def add_rows(total, row_ids, grads):
    selector = (row_ids[:, None] == jnp.arange(total.shape[0], dtype=jnp.int32)[None, :]).astype(
        jnp.float32
    )
    summed = lax.dot_general(
        selector,
        grads,
        (((0,), (0,)), ((), ())),
        precision=lax.Precision.HIGHEST,
        preferred_element_type=jnp.float32,
    )
    return total + summed


def local(
    memory,
    event_feat,
    event_source,
    event_partner,
    event_negative,
    event_time,
    event_count,
    requests,
    w_input,
    w_state,
    w_pair,
    gate_bias,
    time_freq,
):
    node_total = lax.axis_size("node")
    event_total = lax.axis_size("event")
    shards = node_total * event_total
    slots_cap = event_feat.shape[2]
    feat_width = event_feat.shape[3]
    width = memory.shape[1]
    group_rows = memory.shape[0]
    arrived = (
        lax.all_to_all(event_feat, ("node", "event"), split_axis=1, concat_axis=0, tiled=True),
        lax.all_to_all(event_source, ("node", "event"), split_axis=1, concat_axis=0, tiled=True),
        lax.all_to_all(event_partner, ("node", "event"), split_axis=1, concat_axis=0, tiled=True),
        lax.all_to_all(event_negative, ("node", "event"), split_axis=1, concat_axis=0, tiled=True),
        lax.all_to_all(event_time, ("node", "event"), split_axis=1, concat_axis=0, tiled=True),
        lax.all_to_all(event_count, ("node", "event"), split_axis=1, concat_axis=0, tiled=True),
    )
    incoming = lax.all_to_all(requests, "node", split_axis=1, concat_axis=1, tiled=True)
    wanted = incoming.reshape(-1)
    fetched = pick_rows(memory, wanted).reshape(incoming.shape + (width,))
    table = lax.all_to_all(fetched, "node", split_axis=1, concat_axis=1, tiled=True).reshape(
        -1, width
    )
    total_rows = shards * slots_cap
    block_rows = math.gcd(total_rows, 1024)
    turns = total_rows // block_rows
    column = jnp.arange(slots_cap, dtype=jnp.int32)
    valid_all = (column[None, :] < arrived[5]).astype(jnp.float32)
    features = arrived[0].reshape(turns, block_rows, feat_width)
    sources = arrived[1].reshape(turns, block_rows)
    partners = arrived[2].reshape(turns, block_rows)
    negatives = arrived[3].reshape(turns, block_rows)
    timings = arrived[4].reshape(turns, block_rows)
    valids = valid_all.reshape(turns, block_rows)

    def one_block(carry, pieces):
        state_grad, table_grad = carry
        feature, source_ids, partner_ids, negative_ids, time_bins, valid = pieces
        timing = jnp.cos(time_bins.astype(jnp.float32)[:, None] * time_freq[None, :]).astype(
            jnp.bfloat16
        )
        grad_current, grad_partner, grad_negative = pair_grads(
            pick_rows(memory, source_ids),
            pick_rows(table, partner_ids),
            pick_rows(table, negative_ids),
            feature,
            timing,
            valid,
            w_input,
            w_state,
            w_pair,
            gate_bias,
        )
        state_grad = add_rows(state_grad, source_ids, grad_current)
        table_grad = add_rows(
            add_rows(table_grad, partner_ids, grad_partner), negative_ids, grad_negative
        )
        return ((state_grad, table_grad), None)

    start_carry = (
        jnp.zeros((group_rows, width), jnp.float32),
        jnp.zeros((table.shape[0], width), jnp.float32),
    )
    (state_grad, table_grad), _ = lax.scan(
        one_block, start_carry, (features, sources, partners, negatives, timings, valids)
    )
    returned = lax.all_to_all(
        table_grad.reshape(incoming.shape + (width,)),
        "node",
        split_axis=1,
        concat_axis=1,
        tiled=True,
    )
    state_grad = add_rows(state_grad, wanted, returned.reshape(-1, width))
    return lax.psum_scatter(state_grad, "event", scatter_dimension=0, tiled=True)


def solution(mesh):
    in_specs = (
        P("node", None),
        P(("node", "event"), None, None, None),
        P(("node", "event"), None, None),
        P(("node", "event"), None, None),
        P(("node", "event"), None, None),
        P(("node", "event"), None, None),
        P(("node", "event"), None),
        P(("node", "event"), None, None),
        P(),
        P(),
        P(),
        P(),
        P(),
    )
    out_specs = P(("node", "event"), None)
    return jax.shard_map(local, mesh=mesh, in_specs=in_specs, out_specs=out_specs, check_vma=False)
```

profile of v0, /device:TPU:0, one launch (start us, length us, event | category | flops | bytes accessed | tf_op | source)
XLA Modules:
  0.0 309.4 jit_solution(10248121377737930254)
XLA Ops:
  7.3 20.5 %all_to_all.73 = s32[1,128,1]{2,0,1:T(1,128)S(1)} all-to-all(s32[1,128,1]{2,0,1:T(1,128)S(1)} %copy.35), channel_id=1, replica_groups=mesh['node'=8,'event'=16] {'node','event'}, dimensions={1} | all-to-all | bytes 1024 | tf_op jit(solution)/shard_map/all_to_all | solution.py:103
  27.8 3.3 %all-to-all-start.3 = ((s32[1,8,128]{2,0,1:T(1,128)}), s32[1,8,128]{2,0,1:T(1,128)S(1)}, u32[]{:S(2)}, u32[]{:S(2)}) async-start(s32[1,8,128]{2,0,1:T(1,128)} %bitcast.94), calls=%async_computation.3 | async-start | bytes 8192 | tf_op jit(solution)/shard_map/all_to_all | solution.py:105
  32.5 3.7 %all-to-all-done.3 = s32[1,8,128]{2,0,1:T(1,128)S(1)} async-done(((s32[1,8,128]{2,0,1:T(1,128)}), s32[1,8,128]{2,0,1:T(1,128)S(1)}, u32[]{:S(2)}, u32[]{:S(2)}) %all-to-all-start.3) | async-done | bytes 4128 | tf_op jit(solution)/shard_map/all_to_all | solution.py:105
  36.2 4.6 %all-to-all-start = ((s32[1,128,16]{2,0,1:T(1,128)}), s32[1,128,16]{2,0,1:T(1,128)S(1)}, u32[]{:S(2)}, u32[]{:S(2)}) async-start(s32[1,128,16]{2,0,1:T(1,128)} %copy.34), calls=%async_computation | async-start | bytes 131072 | tf_op jit(solution)/shard_map/all_to_all | solution.py:99
  42.3 8.0 %all-to-all-done = s32[1,128,16]{2,0,1:T(1,128)S(1)} async-done(((s32[1,128,16]{2,0,1:T(1,128)}), s32[1,128,16]{2,0,1:T(1,128)S(1)}, u32[]{:S(2)}, u32[]{:S(2)}) %all-to-all-start) | async-done | bytes 8224 | tf_op jit(solution)/shard_map/all_to_all | solution.py:99
  50.3 4.6 %all-to-all-start.2 = ((s32[1,128,16]{2,0,1:T(1,128)}), s32[1,128,16]{2,0,1:T(1,128)S(1)}, u32[]{:S(2)}, u32[]{:S(2)}) async-start(s32[1,128,16]{2,0,1:T(1,128)} %copy.36), calls=%async_computation.2 | async-start | bytes 131072 | tf_op jit(solution)/shard_map/all_to_all | solution.py:100
  56.3 8.1 %all-to-all-done.2 = s32[1,128,16]{2,0,1:T(1,128)S(1)} async-done(((s32[1,128,16]{2,0,1:T(1,128)}), s32[1,128,16]{2,0,1:T(1,128)S(1)}, u32[]{:S(2)}, u32[]{:S(2)}) %all-to-all-start.2) | async-done | bytes 8224 | tf_op jit(solution)/shard_map/all_to_all | solution.py:100
  64.4 4.6 %all-to-all-start.6 = ((s32[1,128,16]{2,0,1:T(1,128)}), s32[1,128,16]{2,0,1:T(1,128)S(1)}, u32[]{:S(2)}, u32[]{:S(2)}) async-start(s32[1,128,16]{2,0,1:T(1,128)} %copy.40), calls=%async_computation.6 | async-start | bytes 131072 | tf_op jit(solution)/shard_map/all_to_all | solution.py:102
  70.4 8.0 %all-to-all-done.6 = s32[1,128,16]{2,0,1:T(1,128)S(1)} async-done(((s32[1,128,16]{2,0,1:T(1,128)}), s32[1,128,16]{2,0,1:T(1,128)S(1)}, u32[]{:S(2)}, u32[]{:S(2)}) %all-to-all-start.6) | async-done | bytes 8224 | tf_op jit(solution)/shard_map/all_to_all | solution.py:102
  78.4 4.6 %all-to-all-start.7 = ((s32[1,128,16]{2,0,1:T(1,128)}), s32[1,128,16]{2,0,1:T(1,128)S(1)}, u32[]{:S(2)}, u32[]{:S(2)}) async-start(s32[1,128,16]{2,0,1:T(1,128)} %copy.41), calls=%async_computation.7 | async-start | bytes 131072 | tf_op jit(solution)/shard_map/all_to_all | solution.py:101
  83.0 2.7 fusion.75
  85.8 6.7 %all-to-all-done.7 = s32[1,128,16]{2,0,1:T(1,128)S(1)} async-done(((s32[1,128,16]{2,0,1:T(1,128)}), s32[1,128,16]{2,0,1:T(1,128)S(1)}, u32[]{:S(2)}, u32[]{:S(2)}) %all-to-all-start.7) | async-done | bytes 8224 | tf_op jit(solution)/shard_map/all_to_all | solution.py:101
  92.5 12.8 %all_to_all.74 = bf16[1,8,128,256]{3,2,0,1:T(8,128)(2,1)S(1)} all-to-all(bf16[1,8,128,256]{3,2,0,1:T(8,128)(2,1)S(1)} %bitcast.85), channel_id=1, replica_groups=mesh['node'=8,'event'=16] {'node'}, dimensions={1} | all-to-all | bytes 1048576 | tf_op jit(solution)/shard_map/all_to_all | solution.py:108
  105.3 4.6 %all-to-all-start.5 = ((bf16[1,128,16,128]{3,2,0,1:T(8,128)(2,1)}), bf16[1,128,16,128]{3,2,0,1:T(8,128)(2,1)S(1)}, u32[]{:S(2)}, u32[]{:S(2)}) async-start(bf16[1,128,16,128]{3,2,0,1:T(8,128)(2,1)} %bitcast.6), calls=%async_computation.5 | async-start | bytes 1048576 | tf_op jit(solution)/shard_map/all_to_all | solution.py:98
  110.0 2.4 reduce.1
  116.8 6.6 %all-to-all-done.5 = bf16[1,128,16,128]{3,2,0,1:T(8,128)(2,1)S(1)} async-done(((bf16[1,128,16,128]{3,2,0,1:T(8,128)(2,1)}), bf16[1,128,16,128]{3,2,0,1:T(8,128)(2,1)S(1)}, u32[]{:S(2)}, u32[]{:S(2)}) %all-to-all-start.5) | async-done | bytes 524320 | tf_op jit(solution)/shard_map/all_to_all | solution.py:98
  123.5 79.2 %while.13 = (s32[]{:T(128)}, f32[2048,256]{1,0:T(8,128)}, f32[1024,256]{1,0:T(8,128)}, s32[2,1024]{1,0:T(2,128)S(1)}, f32[2,1024]{1,0:T(2,128)S(1)}, /*index=5*/...) while((s32[]{:T(128)}, f32[2048,256]{1,0:T(8,128)}, ...), condition=%wide.region_3.4_spmd.clone, body=%wide.region_0.3_spmd.clone.sunk | while | flops 17622900736 | bytes 84141976 | solution.py:151
  127.0 3.8 %fusion.160 = f32[1024,768]{0,1:T(8,128)} fusion(bf16[512,768]{1,0:T(8,128)(2,1)} %get-tuple-element.427, bf16[1024,128]{0,1:T(8,128)(2,1)S(1)} %cosine_convert_fusion.2, bf16[1024,128]{0,1:T(8,128)(2,1)S(1)} %bitcast.80, bf16[1024,256]{0,1:T(8,128)(2,1)S(1)} %fusion.159), kind=kOutput, calls=%fused_computation.54.clone.1 | convolution fusion | flops 808452096 | bytes 4980736 | tf_op jit(solution)/shard_map/while/body/eval_jaxpr/dot_general | solution.py:14
  131.9 3.3 %fusion.156 = bf16[1024,256]{0,1:T(8,128)(2,1)S(1)} fusion(bf16[2048,256]{1,0:T(8,128)(2,1)} %get-tuple-element.428, s32[1024]{0:T(1024)S(1)} %bitcast.88), kind=kOutput, calls=%fused_computation.32.clone.1 | convolution fusion | flops 1076101120 | bytes 1576960 | tf_op jit(solution)/shard_map/while/body/eval_jaxpr/dot_general | solution.py:58
  135.8 3.1 %multiply_reduce_fusion.3 = (f32[1024]{0:T(1024)S(1)}, f32[1024]{0:T(1024)S(1)}, f32[1024,256]{0,1:T(8,128)S(1)}, f32[1024,256]{0,1:T(8,128)S(1)}, f32[1024,256]...) fusion(f32[1024,256]{0,1:T(8,128)S(1)} %fusion.155, bf16[1024,256]{0,1:T(8,128)(2,1)S(1)} %fusion.156, ...), kind=kOutput, calls=%fused_computation.67.clone.1 | convolution fusion | flops 139982848 | bytes 13773824 | tf_op jit(solution)/shard_map/while/body/eval_jaxpr/dot_general | solution.py:27
  143.6 4.6 %fusion.166 = f32[1024,256]{1,0:T(8,128)} fusion(f32[1024,256]{1,0:T(8,128)S(1)} %fusion.165, s32[1024]{0:T(1024)S(1)} %bitcast.93), kind=kOutput, calls=%fused_computation.5.clone.1 | convolution fusion | flops 3222274048 | bytes 2101248 | tf_op jit(solution)/shard_map/while/body/eval_jaxpr/dot_general | solution.py:65
  148.2 6.2 %fusion.169 = f32[1024,256]{1,0:T(8,128)} fusion(f32[1024,256]{1,0:T(8,128)} %fusion.166, f32[1024,256]{1,0:T(8,128)} %fusion.168, s32[1024]{0:T(1024)S(1)} %bitcast.91, f32[1024,256]{1,0:T(8,128)} %get-tuple-element.401, pred[]{:T(512)S(6)} %compare.3), kind=kOutput, calls=%fused_computation.27.clone.1 | convolution fusion | flops 3223060480 | bytes 4198401 | tf_op jit(solution)/shard_map/while/body/eval_jaxpr/dot_general | solution.py:65
  156.1 6.2 %fusion.164 = f32[2048,256]{1,0:T(8,128)} fusion(f32[1024,256]{0,1:T(8,128)S(1)} %fusion.163, s32[1024]{0:T(1024)S(1)} %bitcast.89, f32[2048,256]{1,0:T(8,128)} %get-tuple-element.400, pred[]{:T(512)S(6)} %compare.3), kind=kOutput, calls=%fused_computation.12.clone.1 | convolution fusion | flops 6447693824 | bytes 5246977 | tf_op jit(solution)/shard_map/while/body/eval_jaxpr/dot_general | solution.py:65
  165.6 3.8 %fusion.160 = f32[1024,768]{0,1:T(8,128)} fusion(bf16[512,768]{1,0:T(8,128)(2,1)} %get-tuple-element.427, bf16[1024,128]{0,1:T(8,128)(2,1)S(1)} %cosine_convert_fusion.2, bf16[1024,128]{0,1:T(8,128)(2,1)S(1)} %bitcast.80, bf16[1024,256]{0,1:T(8,128)(2,1)S(1)} %fusion.159), kind=kOutput, calls=%fused_computation.54.clone.1 | convolution fusion | flops 808452096 | bytes 4980736 | tf_op jit(solution)/shard_map/while/body/eval_jaxpr/dot_general | solution.py:14
  170.5 3.3 %fusion.156 = bf16[1024,256]{0,1:T(8,128)(2,1)S(1)} fusion(bf16[2048,256]{1,0:T(8,128)(2,1)} %get-tuple-element.428, s32[1024]{0:T(1024)S(1)} %bitcast.88), kind=kOutput, calls=%fused_computation.32.clone.1 | convolution fusion | flops 1076101120 | bytes 1576960 | tf_op jit(solution)/shard_map/while/body/eval_jaxpr/dot_general | solution.py:58
  174.4 3.1 %multiply_reduce_fusion.3 = (f32[1024]{0:T(1024)S(1)}, f32[1024]{0:T(1024)S(1)}, f32[1024,256]{0,1:T(8,128)S(1)}, f32[1024,256]{0,1:T(8,128)S(1)}, f32[1024,256]...) fusion(f32[1024,256]{0,1:T(8,128)S(1)} %fusion.155, bf16[1024,256]{0,1:T(8,128)(2,1)S(1)} %fusion.156, ...), kind=kOutput, calls=%fused_computation.67.clone.1 | convolution fusion | flops 139982848 | bytes 13773824 | tf_op jit(solution)/shard_map/while/body/eval_jaxpr/dot_general | solution.py:27
  182.2 4.6 %fusion.166 = f32[1024,256]{1,0:T(8,128)} fusion(f32[1024,256]{1,0:T(8,128)S(1)} %fusion.165, s32[1024]{0:T(1024)S(1)} %bitcast.93), kind=kOutput, calls=%fused_computation.5.clone.1 | convolution fusion | flops 3222274048 | bytes 2101248 | tf_op jit(solution)/shard_map/while/body/eval_jaxpr/dot_general | solution.py:65
  186.8 6.5 %fusion.169 = f32[1024,256]{1,0:T(8,128)} fusion(f32[1024,256]{1,0:T(8,128)} %fusion.166, f32[1024,256]{1,0:T(8,128)} %fusion.168, s32[1024]{0:T(1024)S(1)} %bitcast.91, f32[1024,256]{1,0:T(8,128)} %get-tuple-element.401, pred[]{:T(512)S(6)} %compare.3), kind=kOutput, calls=%fused_computation.27.clone.1 | convolution fusion | flops 3223060480 | bytes 4198401 | tf_op jit(solution)/shard_map/while/body/eval_jaxpr/dot_general | solution.py:65
  195.0 7.5 %fusion.164 = f32[2048,256]{1,0:T(8,128)} fusion(f32[1024,256]{0,1:T(8,128)S(1)} %fusion.163, s32[1024]{0:T(1024)S(1)} %bitcast.89, f32[2048,256]{1,0:T(8,128)} %get-tuple-element.400, pred[]{:T(512)S(6)} %compare.3), kind=kOutput, calls=%fused_computation.12.clone.1 | convolution fusion | flops 6447693824 | bytes 5246977 | tf_op jit(solution)/shard_map/while/body/eval_jaxpr/dot_general | solution.py:65
  202.7 19.4 %all_to_all.75 = f32[1,8,128,256]{3,2,0,1:T(8,128)S(1)} all-to-all(f32[1,8,128,256]{3,2,0,1:T(8,128)} %bitcast.82), channel_id=1, replica_groups=mesh['node'=8,'event'=16] {'node'}, dimensions={1} | all-to-all | bytes 2097152 | tf_op jit(solution)/shard_map/all_to_all | solution.py:154
  222.1 9.5 %fusion.74 = f32[2048,256]{1,0:T(8,128)} fusion(f32[2048,256]{1,0:T(8,128)} %get-tuple-element.437, f32[1024,256]{1,0:T(8,128)S(1)} %bitcast.83, s32[1024]{0:T(1024)S(1)} %bitcast.96), kind=kOutput, calls=%fused_computation.94 | convolution fusion | flops 6445072384 | bytes 5246976 | tf_op jit(solution)/shard_map/dot_general | solution.py:65
  231.7 70.8 %reduce-scatter.2.cloned.1.call-done = f32[128,256]{1,0:T(8,128)} async-done(((f32[2048,256]{1,0:T(8,128)}), f32[128,256]{1,0:T(8,128)}) %reduce-scatter.2.cloned.1.call-update) | async-done | bytes 131088 | tf_op jit(solution)/shard_map/reduce_scatter | solution.py:162
  (96 shorter events, 33.4 us)
Async XLA Ops:
  27.8 8.5 %all-to-all-start.3 = ((s32[1,8,128]{2,0,1:T(1,128)}), s32[1,8,128]{2,0,1:T(1,128)S(1)}, u32[]{:S(2)}, u32[]{:S(2)}) async-start(s32[1,8,128]{2,0,1:T(1,128)} %bitcast.94), calls=%async_computation.3 | async-start | bytes 8192 | tf_op jit(solution)/shard_map/all_to_all | solution.py:105
  36.2 14.0 %all-to-all-start = ((s32[1,128,16]{2,0,1:T(1,128)}), s32[1,128,16]{2,0,1:T(1,128)S(1)}, u32[]{:S(2)}, u32[]{:S(2)}) async-start(s32[1,128,16]{2,0,1:T(1,128)} %copy.34), calls=%async_computation | async-start | bytes 131072 | tf_op jit(solution)/shard_map/all_to_all | solution.py:99
  50.3 14.1 %all-to-all-start.2 = ((s32[1,128,16]{2,0,1:T(1,128)}), s32[1,128,16]{2,0,1:T(1,128)S(1)}, u32[]{:S(2)}, u32[]{:S(2)}) async-start(s32[1,128,16]{2,0,1:T(1,128)} %copy.36), calls=%async_computation.2 | async-start | bytes 131072 | tf_op jit(solution)/shard_map/all_to_all | solution.py:100
  64.4 14.0 %all-to-all-start.6 = ((s32[1,128,16]{2,0,1:T(1,128)}), s32[1,128,16]{2,0,1:T(1,128)S(1)}, u32[]{:S(2)}, u32[]{:S(2)}) async-start(s32[1,128,16]{2,0,1:T(1,128)} %copy.40), calls=%async_computation.6 | async-start | bytes 131072 | tf_op jit(solution)/shard_map/all_to_all | solution.py:102
  78.4 14.1 %all-to-all-start.7 = ((s32[1,128,16]{2,0,1:T(1,128)}), s32[1,128,16]{2,0,1:T(1,128)S(1)}, u32[]{:S(2)}, u32[]{:S(2)}) async-start(s32[1,128,16]{2,0,1:T(1,128)} %copy.41), calls=%async_computation.7 | async-start | bytes 131072 | tf_op jit(solution)/shard_map/all_to_all | solution.py:101
  85.7 37.8 %copy-start = (bf16[256,256]{1,0:T(8,128)(2,1)S(1)}, bf16[256,256]{1,0:T(8,128)(2,1)}, u32[]{:S(2)}) copy-start(bf16[256,256]{1,0:T(8,128)(2,1)} %param.25) | copy-start | bytes 393220
  85.7 37.8 %copy-start.2 = (bf16[256,768]{1,0:T(8,128)(2,1)S(1)}, bf16[256,768]{1,0:T(8,128)(2,1)}, u32[]{:S(2)}) copy-start(bf16[256,768]{1,0:T(8,128)(2,1)} %param.24) | copy-start | bytes 1179652
  85.7 37.7 %copy-start.8 = (f32[768]{0:T(1024)S(1)}, f32[768]{0:T(1024)}, u32[]{:S(2)}) copy-start(f32[768]{0:T(1024)} %param.26) | copy-start | bytes 9220
  85.7 37.7 %copy-start.9 = (f32[128]{0:T(128)S(1)}, f32[128]{0:T(128)}, u32[]{:S(2)}) copy-start(f32[128]{0:T(128)} %param.27) | copy-start | bytes 1540
  105.3 18.2 %all-to-all-start.5 = ((bf16[1,128,16,128]{3,2,0,1:T(8,128)(2,1)}), bf16[1,128,16,128]{3,2,0,1:T(8,128)(2,1)S(1)}, u32[]{:S(2)}, u32[]{:S(2)}) async-start(bf16[1,128,16,128]{3,2,0,1:T(8,128)(2,1)} %bitcast.6), calls=%async_computation.5 | async-start | bytes 1048576 | tf_op jit(solution)/shard_map/all_to_all | solution.py:98
  109.9 192.7 %reduce-scatter.2.cloned.1.call-start = ((), (), s32[]{:S(2)}) async-start(), calls=%async_computation.10 | async-start | bytes 2228224 | tf_op jit(solution)/shard_map/reduce_scatter | solution.py:162
  123.7 3.1 copy-start.4
  123.7 7.1 %copy-start.6 = (bf16[1024,256]{1,0:T(8,128)(2,1)}, bf16[1024,256]{1,0:T(8,128)(2,1)S(1)}, u32[]{:S(2)}) copy-start(bf16[1024,256]{1,0:T(8,128)(2,1)S(1)} %get-tuple-element.423) | copy-start | bytes 1572868 | tf_op jit(solution)/shard_map/while
  140.3 1.2 copy-start.10
  148.2 6.2 %copy-start.1 = (bf16[1024,256]{0,1:T(8,128)(2,1)S(1)}, bf16[1024,256]{0,1:T(8,128)(2,1)}, u32[]{:S(2)}) copy-start(bf16[1024,256]{0,1:T(8,128)(2,1)} %get-tuple-element.376) | copy-start | bytes 1572868 | tf_op jit(solution)/shard_map/while
  156.0 6.2 %copy-start.3 = (bf16[256,768]{1,0:T(8,128)(2,1)S(1)}, bf16[256,768]{1,0:T(8,128)(2,1)}, u32[]{:S(2)}) copy-start(bf16[256,768]{1,0:T(8,128)(2,1)} %get-tuple-element.454) | copy-start | bytes 1179652 | tf_op jit(solution)/shard_map/while
  156.1 6.2 %copy-start.5 = (bf16[2,1024,128]{2,1,0:T(8,128)(2,1)S(1)}, bf16[2,1024,128]{2,1,0:T(8,128)(2,1)}, u32[]{:S(2)}) copy-start(bf16[2,1024,128]{2,1,0:T(8,128)(2,1)} %copy-done.4) | copy-start | bytes 1572868 | tf_op jit(solution)/shard_map/while
  156.1 6.2 %copy-start.7 = (bf16[1024,256]{1,0:T(8,128)(2,1)S(1)}, bf16[1024,256]{1,0:T(8,128)(2,1)}, u32[]{:S(2)}) copy-start(bf16[1024,256]{1,0:T(8,128)(2,1)} %copy-done.6) | copy-start | bytes 1572868 | tf_op jit(solution)/shard_map/while
  162.3 3.1 copy-start.4
  162.3 7.1 %copy-start.6 = (bf16[1024,256]{1,0:T(8,128)(2,1)}, bf16[1024,256]{1,0:T(8,128)(2,1)S(1)}, u32[]{:S(2)}) copy-start(bf16[1024,256]{1,0:T(8,128)(2,1)S(1)} %get-tuple-element.423) | copy-start | bytes 1572868 | tf_op jit(solution)/shard_map/while
  178.9 1.2 copy-start.10
  186.8 6.6 %copy-start.1 = (bf16[1024,256]{0,1:T(8,128)(2,1)S(1)}, bf16[1024,256]{0,1:T(8,128)(2,1)}, u32[]{:S(2)}) copy-start(bf16[1024,256]{0,1:T(8,128)(2,1)} %get-tuple-element.376) | copy-start | bytes 1572868 | tf_op jit(solution)/shard_map/while
  194.9 7.5 %copy-start.3 = (bf16[256,768]{1,0:T(8,128)(2,1)S(1)}, bf16[256,768]{1,0:T(8,128)(2,1)}, u32[]{:S(2)}) copy-start(bf16[256,768]{1,0:T(8,128)(2,1)} %get-tuple-element.454) | copy-start | bytes 1179652 | tf_op jit(solution)/shard_map/while
  195.0 7.5 %copy-start.5 = (bf16[2,1024,128]{2,1,0:T(8,128)(2,1)S(1)}, bf16[2,1024,128]{2,1,0:T(8,128)(2,1)}, u32[]{:S(2)}) copy-start(bf16[2,1024,128]{2,1,0:T(8,128)(2,1)} %copy-done.4) | copy-start | bytes 1572868 | tf_op jit(solution)/shard_map/while
  195.0 7.5 %copy-start.7 = (bf16[1024,256]{1,0:T(8,128)(2,1)S(1)}, bf16[1024,256]{1,0:T(8,128)(2,1)}, u32[]{:S(2)}) copy-start(bf16[1024,256]{1,0:T(8,128)(2,1)} %copy-done.6) | copy-start | bytes 1572868 | tf_op jit(solution)/shard_map/while
Sparse Core Ops, SparseCore 0:
  231.8 70.6 reduce-scatter.1
where the time goes:
time: 310 us; the launch traced here: 309 us
  waiting for transfers between devices  112 us (36%)
  matrix products  82.1 us (26%)
  blocking collectives  52.7 us (17%)
  starting transfers between devices  26.3 us (8%)
  other arithmetic  13.6 us (4%)
  between operations  13.6 us (4%)
  local copies, waits for them, and re-layouts  8.22 us (3%)
    reduce_scatter x1, waiting for transfers between devices, local(): lax.psum_scatter(state_grad, 'event', scatter_dimension=0, tiled=True)  70.8 us
    dot_general x7, matrix products, add_rows(): lax.dot_general(selector, grads, (((0,), (0,)), ((), ())), precision=lax....  45.2 us
    all_to_all x1, blocking collectives, local(): lax.all_to_all(event_count, ('node', 'event'), split_axis=1, concat_axis=...  20.5 us
    all_to_all x1, blocking collectives, local(): lax.all_to_all(table_grad.reshape(incoming.shape + (width,)), 'node', spl...  19.4 us
    all_to_all x1, blocking collectives, local(): lax.all_to_all(fetched, 'node', split_axis=1, concat_axis=1, tiled=True)  12.8 us
    dot_general x5, matrix products, pick_rows(): jnp.dot(selector, values, preferred_element_type=jnp.float32)  11.5 us
    all_to_all x1, waiting for transfers between devices, local(): lax.all_to_all(event_partner, ('node', 'event'), split_axis=1, concat_axi...  8.08 us
    all_to_all x1, waiting for transfers between devices, local(): lax.all_to_all(event_source, ('node', 'event'), split_axis=1, concat_axis...  8.01 us
  transfers between devices with their start and end apart: 7, of which 7 were waited for; matrix products, arithmetic and copies ran while one was open for 5% of the time, Pallas kernels for 0%

commit v1 on v0

v1 whole, which is shorter than its diff:
```python
import functools

import jax
import jax.numpy as jnp
from jax import lax
from jax.experimental import pallas as pl
from jax.experimental.pallas import tpu as pltpu
from jax.sharding import PartitionSpec as P

F32 = jnp.float32
BF16 = jnp.bfloat16


def dot(a, b):
    return jnp.dot(a, b, preferred_element_type=F32)


def dot_nt(a, b):
    return lax.dot_general(a, b, (((1,), (1,)), ((), ())), preferred_element_type=F32)


def iota(shape, dim):
    return lax.broadcasted_iota(jnp.int32, shape, dim)


def split(x):
    high = x.astype(BF16)
    low = (x - high.astype(F32)).astype(BF16)
    return high, low


def call(kernel, outs, args, grid=None, in_specs=None, out_specs=None, scratch=(), flops=0, moved=0, trans=0, name=None, prefetch=0):
    spec = pltpu.PrefetchScalarGridSpec(
        num_scalar_prefetch=prefetch,
        grid=grid or (1,),
        in_specs=in_specs,
        out_specs=out_specs,
        scratch_shapes=list(scratch),
    )
    return pl.pallas_call(
        kernel,
        out_shape=outs,
        grid_spec=spec,
        name=name,
        compiler_params=pltpu.CompilerParams(vmem_limit_bytes=48 << 20),
        cost_estimate=pl.CostEstimate(flops=int(flops), bytes_accessed=int(moved), transcendentals=int(trans)),
    )(*args)


def whole(shape):
    return pl.BlockSpec(shape, lambda *_: (0,) * len(shape))


def pack_kernel(group_rows, table_rows, feat, source, partner, negative, time, count, wanted, out):
    shards, slots, width = feat.shape
    groups = wanted.shape[0]
    live = iota((slots, shards), 0) < count[...]
    fields = (
        jnp.where(live, source[...], group_rows),
        jnp.where(live, partner[...], table_rows),
        jnp.where(live, negative[...], table_rows),
        time[...],
    )
    parts = []
    for field in fields:
        parts += [(field >> 8).astype(F32), (field & 255).astype(F32)]
    ids = jnp.concatenate(parts, axis=0).T
    rows = (shards, 8, width)

    def spread(x):
        return jnp.broadcast_to(x[:, None, :], rows)

    def by_group(x):
        return jnp.broadcast_to(x[:, None, :], (groups, shards // groups, width)).reshape(shards, width)

    place = iota(rows, 1)
    high = by_group((wanted[...] >> 8).astype(F32))
    low = by_group((wanted[...] & 255).astype(F32))
    tail = jnp.where(place == 0, spread(ids), jnp.where(place == 1, spread(high), spread(low)))
    out[:, 0:slots, :] = feat[...]
    out[:, slots : slots + 8, :] = tail.astype(BF16)


def field_columns(tail, field):
    blocks = tail.shape[0]
    row = tail[...].astype(F32)[:, 0:1, :]
    spread = jnp.broadcast_to(row, (blocks, 16, 128)).reshape(blocks * 16, 128)
    shape = (blocks * 16, 128)
    masked = jnp.where((iota(shape, 1) & 15) == (iota(shape, 0) & 15), spread, 0.0).astype(BF16)
    lane = iota((128, 128), 0) >> 4
    weight = jnp.where(lane == 2 * field, 256.0, jnp.where(lane == 2 * field + 1, 1.0, 0.0)).astype(BF16)
    return masked, weight


def columns_of(masked, weight):
    return dot(masked, weight)


def rows_of(masked, weight):
    return dot_nt(weight.T[0:8, :], masked)


def one_hot_columns(values, count):
    rows = values.shape[0]
    ids = values.astype(jnp.int32)
    pieces = [
        jnp.where(iota((rows, 128), 1) == ids - 128 * t, 1.0, 0.0).astype(BF16) for t in range(count // 128)
    ]
    return jnp.concatenate(pieces, axis=1)


def one_hot_rows(values, count, start=0):
    shape = (count, values.shape[1])
    ids = jnp.broadcast_to(values.astype(jnp.int32) - start, shape)
    return jnp.where(iota(shape, 0) == ids, 1.0, 0.0).astype(BF16)


def wanted_values(tail):
    rows = tail[...].astype(F32)[:, 0]
    return rows[:, 1], rows[:, 2]


def fetch_kernel(place, tail, memory, out):
    high, low = wanted_values(tail)
    groups = high.shape[0]
    shape = (groups * 128, 128)
    here = iota(shape, 1) == (iota(shape, 0) & 127)

    def spread(x):
        wide = jnp.broadcast_to(x[:, None, :], (groups, 128, 128)).reshape(shape)
        return jnp.where(here, wide, 0.0).astype(BF16)

    joined = jnp.concatenate([spread(high), spread(low)], axis=1)
    weight = jnp.where(iota((256, 128), 0) < 128, 256.0, 1.0).astype(BF16)
    values = dot(joined, weight)
    selector = one_hot_columns(values, memory.shape[0])
    out[...] = dot(selector, memory[...]).astype(BF16)


def source_kernel(tail, memory, freq, current, timing, rows):
    masked, weight = field_columns(tail, 0)
    values = columns_of(masked, weight)
    rows[...] = rows_of(masked, weight)
    selector = one_hot_columns(values, memory.shape[0])
    current[...] = dot(selector, memory[...]).astype(BF16)
    _, weight = field_columns(tail, 3)
    timing[...] = jnp.cos(columns_of(masked, weight) * freq[...]).astype(BF16)


def step_kernel(message, table, current_ref, timing, w_input, w_state, w_pair, bias, table_grad, grad_high, grad_low, acc, acc_neg):
    at = pl.program_id(0)
    table_rows, width = table.shape
    blocks = message.shape[0]
    events = blocks * 16
    feature = message[:, 0:16, :].reshape(events, 128)
    tail = message[:, 16:24, :]
    masked, weight_p = field_columns(tail, 1)
    _, weight_n = field_columns(tail, 2)
    partner = dot(one_hot_columns(columns_of(masked, weight_p), table_rows), table[...]).astype(BF16)
    negative = dot(one_hot_columns(columns_of(masked, weight_n), table_rows), table[...]).astype(BF16)
    current = current_ref[...]
    joined = jnp.concatenate([partner, feature, timing[...]], axis=1)
    w_in = w_input[...]
    from_input = dot(joined, w_in)
    from_state = dot(current, w_state[...])
    gate = bias[...]
    reset = jax.nn.sigmoid(from_input[:, :width] + from_state[:, :width] + gate[:, :width])
    update = jax.nn.sigmoid(
        from_input[:, width : 2 * width] + from_state[:, width : 2 * width] + gate[:, width : 2 * width]
    )
    recurrent = from_state[:, 2 * width :]
    candidate = jnp.tanh(from_input[:, 2 * width :] + gate[:, 2 * width :] + reset * recurrent)
    previous = current.astype(F32)
    renewed = (1.0 - update) * candidate + update * previous
    factor = 1.0 / width**0.5
    key_pos = dot(partner, w_pair[...])
    key_neg = dot(negative, w_pair[...])
    score_pos = jnp.sum(renewed * key_pos, axis=1, keepdims=True) * factor
    score_neg = jnp.sum(renewed * key_neg, axis=1, keepdims=True) * factor
    weight_pos = -jax.nn.sigmoid(-score_pos)
    weight_neg = jax.nn.sigmoid(score_neg)
    grad_renewed = (weight_pos * key_pos + weight_neg * key_neg) * factor
    grad_keypos = (weight_pos * renewed * factor).astype(BF16)
    grad_keyneg = (weight_neg * renewed * factor).astype(BF16)
    grad_cand = grad_renewed * (1.0 - update) * (1.0 - candidate * candidate)
    grad_reset = grad_cand * recurrent * reset * (1.0 - reset)
    grad_update = grad_renewed * (previous - candidate) * update * (1.0 - update)
    first = grad_reset.astype(BF16)
    second = grad_update.astype(BF16)
    input_back = jnp.concatenate([first, second, grad_cand.astype(BF16)], axis=1)
    state_back = jnp.concatenate([first, second, (grad_cand * reset).astype(BF16)], axis=1)
    grad_current = grad_renewed * update + dot_nt(state_back, w_state[...])
    high, low = split(grad_current)
    grad_high[...] = high
    grad_low[...] = low
    grad_partner = dot_nt(input_back, w_in[:width, :]) + dot_nt(grad_keypos, w_pair[...])
    high, low = split(grad_partner)
    to_partner = one_hot_rows(rows_of(masked, weight_p)[0:1, :], table_rows)
    to_negative = one_hot_rows(rows_of(masked, weight_n)[0:1, :], table_rows)
    added = dot(to_partner, high) + dot(to_partner, low)
    added_neg = dot(to_negative, grad_keyneg)

    @pl.when(at == 0)
    def _():
        acc[...] = added
        acc_neg[...] = added_neg

    @pl.when(at > 0)
    def _():
        acc[...] += added
        acc_neg[...] += added_neg

    @pl.when(at == pl.num_programs(0) - 1)
    def _():
        high, low = split(acc_neg[...])
        total = acc[...] + dot_nt(high, w_pair[...]) + dot_nt(low, w_pair[...])
        table_grad[...] = total.astype(BF16)


def source_scatter_kernel(rows, grad_high, grad_low, out):
    count = out.shape[0]
    selector = one_hot_rows(rows[0:1, :], count, pl.program_id(0) * count)
    out[...] = dot(selector, grad_high[...]) + dot(selector, grad_low[...])


def returned_kernel(place, tail, returned, state_grad, out):
    high, low = wanted_values(tail)
    values = high * 256.0 + low
    count = out.shape[0]
    start = pl.program_id(0) * count
    pieces = [one_hot_rows(values[g : g + 1, :], count, start) for g in range(values.shape[0])]
    selector = jnp.concatenate(pieces, axis=1)
    out[...] = (state_grad[...] + dot(selector, returned[...])).astype(BF16)


def local(
    memory,
    event_feat,
    event_source,
    event_partner,
    event_negative,
    event_time,
    event_count,
    requests,
    w_input,
    w_state,
    w_pair,
    gate_bias,
    time_freq,
):
    nodes = lax.axis_size("node")
    peers = lax.axis_size("event")
    shards = nodes * peers
    group_rows, width = memory.shape
    _, groups, per_group = requests.shape
    table_rows = groups * per_group
    slots, feat_width = event_feat.shape[2:]
    events = shards * slots

    flat = [x[0].T for x in (event_source, event_partner, event_negative, event_time)]
    args = (event_feat[0], *flat, event_count, requests[0])
    message = call(
        functools.partial(pack_kernel, group_rows, table_rows),
        jax.ShapeDtypeStruct((shards, slots + 8, feat_width), BF16),
        args,
        in_specs=[whole(x.shape) for x in args],
        out_specs=whole((shards, slots + 8, feat_width)),
        moved=2 * events * feat_width * 2,
        name="pack",
    )
    message = lax.all_to_all(message, ("node", "event"), 0, 0, tiled=True)
    place = lax.axis_index("event").astype(jnp.int32).reshape(1)
    by_peer = message.reshape(nodes, peers, slots + 8, feat_width)
    tail_spec = pl.BlockSpec((nodes, 1, 8, feat_width), lambda i, at: (0, at[0], slots // 8, 0))
    fetched = call(
        fetch_kernel,
        jax.ShapeDtypeStruct((table_rows, width), BF16),
        (place, by_peer, memory),
        in_specs=[tail_spec, whole(memory.shape)],
        out_specs=whole((table_rows, width)),
        flops=2 * table_rows * group_rows * width,
        moved=group_rows * width * 2,
        name="fetch",
        prefetch=1,
    )
    table = lax.all_to_all(fetched.reshape(groups, per_group, width), "node", 0, 0, tiled=True).reshape(table_rows, width)

    block = 512
    turns = events // block
    rows_block = lambda i: (i, 0)
    current, timing, rows = call(
        source_kernel,
        (
            jax.ShapeDtypeStruct((events, width), BF16),
            jax.ShapeDtypeStruct((events, feat_width), BF16),
            jax.ShapeDtypeStruct((8, events), F32),
        ),
        (message, memory, time_freq.reshape(1, -1)),
        grid=(turns,),
        in_specs=[
            pl.BlockSpec((block // slots, 8, feat_width), lambda i: (i, slots // 8, 0)),
            whole(memory.shape),
            whole((1, feat_width)),
        ],
        out_specs=(
            pl.BlockSpec((block, width), rows_block),
            pl.BlockSpec((block, feat_width), rows_block),
            pl.BlockSpec((8, block), lambda i: (0, i)),
        ),
        flops=2 * events * group_rows * width,
        moved=4 * events * width,
        trans=events * feat_width,
        name="source",
    )
    table_grad, grad_high, grad_low = call(
        step_kernel,
        (
            jax.ShapeDtypeStruct((table_rows, width), BF16),
            jax.ShapeDtypeStruct((events, width), BF16),
            jax.ShapeDtypeStruct((events, width), BF16),
        ),
        (message, table, current, timing, w_input, w_state, w_pair, gate_bias.reshape(1, -1)),
        grid=(turns,),
        in_specs=[
            pl.BlockSpec((block // slots, slots + 8, feat_width), lambda i: (i, 0, 0)),
            whole(table.shape),
            pl.BlockSpec((block, width), rows_block),
            pl.BlockSpec((block, feat_width), rows_block),
            whole(w_input.shape),
            whole(w_state.shape),
            whole(w_pair.shape),
            whole((1, 3 * width)),
        ],
        out_specs=(
            whole((table_rows, width)),
            pl.BlockSpec((block, width), rows_block),
            pl.BlockSpec((block, width), rows_block),
        ),
        scratch=[pltpu.VMEM((table_rows, width), F32), pltpu.VMEM((table_rows, width), F32)],
        flops=2 * events * width * (5 * table_rows + 3 * 4 * width + 3 * 3 * width),
        moved=8 * events * width,
        trans=events * width * 3,
        name="step",
    )
    returned = lax.all_to_all(table_grad.reshape(groups, per_group, width), "node", 0, 0, tiled=True).reshape(table_rows, width)
    node_block = 512
    state_grad = call(
        source_scatter_kernel,
        jax.ShapeDtypeStruct((group_rows, width), F32),
        (rows, grad_high, grad_low),
        grid=(group_rows // node_block,),
        in_specs=[whole(rows.shape), whole(grad_high.shape), whole(grad_low.shape)],
        out_specs=pl.BlockSpec((node_block, width), rows_block),
        flops=4 * events * group_rows * width,
        moved=8 * events * width,
        name="scatter",
    )
    total = call(
        returned_kernel,
        jax.ShapeDtypeStruct((group_rows, width), BF16),
        (place, by_peer, returned, state_grad),
        grid=(group_rows // node_block,),
        in_specs=[
            tail_spec,
            pl.BlockSpec((table_rows, width), lambda i, at: (0, 0)),
            pl.BlockSpec((node_block, width), lambda i, at: (i, 0)),
        ],
        out_specs=pl.BlockSpec((node_block, width), lambda i, at: (i, 0)),
        flops=2 * table_rows * group_rows * width,
        moved=6 * group_rows * width,
        name="returned",
        prefetch=1,
    )
    shares = lax.all_to_all(total.reshape(peers, group_rows // peers, width), "event", 0, 0, tiled=True)
    return jnp.sum(shares.astype(F32), axis=0)


def solution(mesh):
    in_specs = (
        P("node", None),
        P(("node", "event"), None, None, None),
        P(("node", "event"), None, None),
        P(("node", "event"), None, None),
        P(("node", "event"), None, None),
        P(("node", "event"), None, None),
        P(("node", "event"), None),
        P(("node", "event"), None, None),
        P(),
        P(),
        P(),
        P(),
        P(),
    )
    out_specs = P(("node", "event"), None)
    return jax.shard_map(local, mesh=mesh, in_specs=in_specs, out_specs=out_specs, check_vma=False)
```

time: 310 us -> 109 us (0.35)
  waiting for transfers between devices: 112 us -> 19.4 us
  matrix products: 82.1 us -> 0 us
  Pallas kernels: 0 us -> 34.4 us
  blocking collectives: 52.7 us -> 19.9 us
  between operations: 13.6 us -> 0.12 us
  other arithmetic: 13.6 us -> 0.79 us
  starting transfers between devices: 26.3 us -> 18.3 us
  local copies, waits for them, and re-layouts: 8.22 us -> 14.8 us
    dot_general x28 -> x0, matrix products: 82.1 us -> none  [the longest x7 45.2 us: add_rows(): lax.dot_general(selector, grads, (((0,), (0,)), ((), ())), precision=lax....]
    reduce_scatter x1 -> x0, waiting for transfers between devices: 70.8 us -> none  [local(): lax.psum_scatter(state_grad, 'event', scatter_dimension=0, tiled=True)]
    pallas_call x0 -> x6, Pallas kernels: none -> 34.4 us  [call(): pl.pallas_call(kernel, out_shape=outs, grid_spec=spec, name=name, compile...]
    all_to_all x3 -> x1, blocking collectives: 52.7 us -> 19.9 us  [local(): lax.all_to_all(total.reshape(peers, group_rows // peers, width), 'event',...]
    all_to_all x6 -> x3, waiting for transfers between devices: 41.2 us -> 19.4 us  [the longest x1 16.3 us: local(): message = lax.all_to_all(message, ('node', 'event'), 0, 0, tiled=True)]
    unnamed x12 -> x44, local copies, waits for them, and re-layouts: 5.73 us -> 14.8 us
    all_to_all x6 -> x3, starting transfers between devices: 26.3 us -> 18.3 us  [the longest x1 11.2 us: local(): message = lax.all_to_all(message, ('node', 'event'), 0, 0, tiled=True)]
    all_to_all x5 -> x0, other arithmetic: 5.52 us -> none  [the longest x1 2.35 us: local(): lax.all_to_all(event_count, ('node', 'event'), split_axis=1, concat_axis=...]
  transfers between devices with their start and end apart: 7 -> 3, of which waited for: 7 -> 3; matrix products, arithmetic and copies ran while one was open for 5% -> 0% of each run, Pallas kernels for 0% -> 11%
where the time goes in v1:
time: 109 us; the launch traced here: 108 us
  Pallas kernels  34.4 us (32%)
  blocking collectives  19.9 us (18%)
  waiting for transfers between devices  19.4 us (18%)
  starting transfers between devices  18.3 us (17%)
  local copies, waits for them, and re-layouts  14.8 us (14%)
    pallas_call x6, Pallas kernels, call(): pl.pallas_call(kernel, out_shape=outs, grid_spec=spec, name=name, compile...  34.4 us
    all_to_all x1, blocking collectives, local(): lax.all_to_all(total.reshape(peers, group_rows // peers, width), 'event',...  19.9 us
    all_to_all x1, waiting for transfers between devices, local(): message = lax.all_to_all(message, ('node', 'event'), 0, 0, tiled=True)  16.3 us
    unnamed x44, local copies, waits for them, and re-layouts  14.8 us
    all_to_all x1, starting transfers between devices, local(): message = lax.all_to_all(message, ('node', 'event'), 0, 0, tiled=True)  11.2 us
    all_to_all x1, starting transfers between devices, local(): lax.all_to_all(table_grad.reshape(groups, per_group, width), 'node', 0, 0...  3.66 us
    all_to_all x1, starting transfers between devices, local(): lax.all_to_all(fetched.reshape(groups, per_group, width), 'node', 0, 0, t...  3.49 us
  transfers between devices with their start and end apart: 3, of which 3 were waited for; matrix products, arithmetic and copies ran while one was open for 0% of the time, Pallas kernels for 11%

profile of v1, /device:TPU:0, one launch (start us, length us, event | category | flops | bytes accessed | tf_op | source)
XLA Modules:
  0.0 107.7 jit_solution(7774874441672481042)
XLA Ops:
  0.0 1.0 copy-done
  1.0 0.7 copy-done.1
  1.7 0.7 copy-done.2
  2.4 0.7 copy-done.3
  3.1 0.7 copy-done.4
  3.8 0.7 copy-done.5
  4.5 0.7 copy-done.6
  5.2 1.1 pack.1
  6.2 11.2 %all-to-all-start = ((bf16[128,24,128]{2,1,0:T(8,128)(2,1)}), bf16[128,24,128]{2,1,0:T(8,128)(2,1)S(1)}, u32[]{:S(2)}, u32[]{:S(2)}) async-start(bf16[128,24,128]{2,1,0:T(8,128)(2,1)} %pack.1), calls=%async_computation | async-start | bytes 1572864 | tf_op jit(solution)/shard_map/all_to_all | solution.py:271
  17.4 16.3 %all-to-all-done.tail.message = bf16[128,24,128]{2,1,0:T(8,128)(2,1)S(1)} async-done(((bf16[128,24,128]{2,1,0:T(8,128)(2,1)}), bf16[128,24,128]{2,1,0:T(8,128)(2,1)S(1)}, u32[]{:S(2)}, u32[]{:S(2)}) %all-to-all-start) | async-done | bytes 786464 | tf_op jit(solution)/shard_map/all_to_all | solution.py:271
  33.7 2.4 %fetch.1 = bf16[1024,256]{1,0:T(8,128)(2,1)} custom-call(s32[1]{0:T(128)} %bitcast.place, bf16[8,16,24,128]{3,2,1,0:T(8,128)(2,1)S(1)} %bitcast.23, bf16[2048,256]{1,0:T(8,128)(2,1)S(1)} %copy-done.7), custom_call_target="tpu_custom_call" | custom-call | flops 1073741824 | bytes 1048576 | tf_op jit(solution)/shard_map/fetch/pallas_call | solution.py:40
  36.2 3.5 %all-to-all-start.1 = ((bf16[8,128,256]{2,1,0:T(8,128)(2,1)}), bf16[8,128,256]{2,1,0:T(8,128)(2,1)S(1)}, u32[]{:S(2)}, u32[]{:S(2)}) async-start(bf16[8,128,256]{2,1,0:T(8,128)(2,1)} %bitcast.12), calls=%async_computation.1 | async-start | bytes 1048576 | tf_op jit(solution)/shard_map/all_to_all | solution.py:286
  39.7 0.0 copy-start.9
  39.7 6.7 %source.1 = (bf16[2048,256]{1,0:T(8,128)(2,1)S(1)}, bf16[2048,128]{1,0:T(8,128)(2,1)S(1)}, f32[8,2048]{1,0:T(8,128)S(1)}) custom-call(bf16[128,24,128]{2,1,0:T(8,128)(2,1)S(1)} %all-to-all-done.tail.message, bf16[2048,256]{1,0:T(8,128)(2,1)S(1)} %copy-done.7, f32[1,128]{1,0:T(1,128)S(1)} %bitcast.33), custom_call_target="tpu_custom_call" | custom-call | flops 2147483648 | bytes 2097152 | tf_op jit(solution)/shard_map/source/pallas_call | solution.py:40
  46.4 1.0 copy-done.12
  47.4 0.8 copy-done.13
  48.2 0.6 copy-done.19
  48.9 1.1 all-to-all-done.1
  49.9 0.9 copy-done.10
  50.8 1.0 copy-done.14
  51.9 17.3 %step.1 = (bf16[1024,256]{1,0:T(8,128)(2,1)}, bf16[2048,256]{1,0:T(8,128)(2,1)S(1)}, bf16[2048,256]{1,0:T(8,128)(2,1)S(1)}) custom-call(bf16[128,24,128]{2,1,0:T(8,128)(2,1)S(1)} %all-to-all-done.tail.message, bf16[1024,256]{1,0:T(8,128)(2,1)S(1)} %bitcast.27, bf16[2048,256]{1,0:T(8,128)(2,1)} %copy-done.12, bf16[2048,128]{1,0:T(8,128)(2,1)S(1)} %copy-done.14, ...), custom_call_target="tpu_custom_call" | custom-call | flops 11005853696 | bytes 4194304 | tf_op jit(solution)/shard_map/step/pallas_call | solution.py:40
  69.2 1.0 copy-done.15
  70.2 0.9 copy-done.17
  71.2 3.7 %all-to-all-start.2 = ((bf16[8,128,256]{2,1,0:T(8,128)(2,1)}), bf16[8,128,256]{2,1,0:T(8,128)(2,1)S(1)}, u32[]{:S(2)}, u32[]{:S(2)}) async-start(bf16[8,128,256]{2,1,0:T(8,128)(2,1)} %bitcast.15), calls=%async_computation.2 | async-start | bytes 1048576 | tf_op jit(solution)/shard_map/all_to_all | solution.py:345
  74.8 1.2 %copy-done.16 = bf16[2048,256]{1,0:T(8,128)(2,1)S(1)} copy-done((bf16[2048,256]{1,0:T(8,128)(2,1)S(1)}, bf16[2048,256]{1,0:T(8,128)(2,1)}, u32[]{:S(2)}) %copy-start.16) | copy-done | bytes 1048600
  76.1 1.2 %copy-done.18 = bf16[2048,256]{1,0:T(8,128)(2,1)S(1)} copy-done((bf16[2048,256]{1,0:T(8,128)(2,1)S(1)}, bf16[2048,256]{1,0:T(8,128)(2,1)}, u32[]{:S(2)}) %copy-start.18) | copy-done | bytes 1048600
  77.3 0.8 copy-done.20
  78.1 5.0 %scatter.1.state_grad = f32[2048,256]{1,0:T(8,128)S(1)} custom-call(f32[8,2048]{1,0:T(8,128)S(1)} %copy-done.20, bf16[2048,256]{1,0:T(8,128)(2,1)S(1)} %copy-done.16, bf16[2048,256]{1,0:T(8,128)(2,1)S(1)} %copy-done.18), custom_call_target="tpu_custom_call" | custom-call | flops 4294967296 | bytes 4194304 | tf_op jit(solution)/shard_map/scatter/pallas_call | solution.py:40
  83.1 2.0 %all-to-all-done.2 = bf16[8,128,256]{2,1,0:T(8,128)(2,1)S(1)} async-done(((bf16[8,128,256]{2,1,0:T(8,128)(2,1)}), bf16[8,128,256]{2,1,0:T(8,128)(2,1)S(1)}, u32[]{:S(2)}, u32[]{:S(2)}) %all-to-all-start.2) | async-done | bytes 524320 | tf_op jit(solution)/shard_map/all_to_all | solution.py:345
  85.1 1.8 %returned.1 = bf16[2048,256]{1,0:T(8,128)(2,1)S(1)} custom-call(s32[1]{0:T(128)} %bitcast.place, bf16[8,16,24,128]{3,2,1,0:T(8,128)(2,1)S(1)} %bitcast.24, bf16[1024,256]{1,0:T(8,128)(2,1)S(1)} %bitcast.25, f32[2048,256]{1,0:T(8,128)S(1)} %scatter.1.state_grad), custom_call_target="tpu_custom_call" | custom-call | flops 1073741824 | bytes 3145728 | tf_op jit(solution)/shard_map/returned/pallas_call | solution.py:40
  87.0 19.9 %all_to_all.20 = bf16[16,128,256]{2,1,0:T(8,128)(2,1)S(1)} all-to-all(bf16[16,128,256]{2,1,0:T(8,128)(2,1)S(1)} %bitcast.22), channel_id=1, replica_groups=mesh['node'=8,'event'=16] {'event'}, dimensions={0} | all-to-all | bytes 2097152 | tf_op jit(solution)/shard_map/all_to_all | solution.py:374
  106.9 0.8 convert_reduce_fusion
  (27 shorter events, 0.1 us)
Async XLA Ops:
  0.0 1.0 copy-start
  1.0 0.7 copy-start.1
  1.7 0.7 copy-start.2
  2.4 0.7 copy-start.3
  3.1 0.7 copy-start.4
  3.8 0.7 copy-start.5
  4.5 0.7 copy-start.6
  5.2 28.5 %copy-start.7 = (bf16[2048,256]{1,0:T(8,128)(2,1)S(1)}, bf16[2048,256]{1,0:T(8,128)(2,1)}, u32[]{:S(2)}) copy-start(bf16[2048,256]{1,0:T(8,128)(2,1)} %memory.3) | copy-start | bytes 3145732
  6.2 27.5 %all-to-all-start = ((bf16[128,24,128]{2,1,0:T(8,128)(2,1)}), bf16[128,24,128]{2,1,0:T(8,128)(2,1)S(1)}, u32[]{:S(2)}, u32[]{:S(2)}) async-start(bf16[128,24,128]{2,1,0:T(8,128)(2,1)} %pack.1), calls=%async_computation | async-start | bytes 1572864 | tf_op jit(solution)/shard_map/all_to_all | solution.py:271
  33.7 6.0 %copy-start.21 = (f32[768]{0:T(1024)S(1)}, f32[768]{0:T(1024)}, u32[]{:S(2)}) copy-start(f32[768]{0:T(1024)} %param.24) | copy-start | bytes 9220
  33.7 6.0 %copy-start.11 = (f32[128]{0:T(128)S(1)}, f32[128]{0:T(128)}, u32[]{:S(2)}) copy-start(f32[128]{0:T(128)} %param.25) | copy-start | bytes 1540
  36.2 13.7 %all-to-all-start.1 = ((bf16[8,128,256]{2,1,0:T(8,128)(2,1)}), bf16[8,128,256]{2,1,0:T(8,128)(2,1)S(1)}, u32[]{:S(2)}, u32[]{:S(2)}) async-start(bf16[8,128,256]{2,1,0:T(8,128)(2,1)} %bitcast.12), calls=%async_computation.1 | async-start | bytes 1048576 | tf_op jit(solution)/shard_map/all_to_all | solution.py:286
  39.7 10.2 %copy-start.8 = (bf16[512,768]{1,0:T(8,128)(2,1)S(1)}, bf16[512,768]{1,0:T(8,128)(2,1)}, u32[]{:S(2)}) copy-start(bf16[512,768]{1,0:T(8,128)(2,1)} %w_input.1) | copy-start | bytes 2359300
  39.7 10.2 %copy-start.9 = (bf16[256,768]{1,0:T(8,128)(2,1)S(1)}, bf16[256,768]{1,0:T(8,128)(2,1)}, u32[]{:S(2)}) copy-start(bf16[256,768]{1,0:T(8,128)(2,1)} %w_state.1) | copy-start | bytes 1179652
  46.4 1.0 copy-start.12
  47.4 0.8 copy-start.13
  48.2 0.6 copy-start.19
  49.9 0.9 copy-start.10
  50.8 1.0 copy-start.14
  69.2 1.0 copy-start.15
  70.2 0.9 copy-start.17
  71.2 14.0 %all-to-all-start.2 = ((bf16[8,128,256]{2,1,0:T(8,128)(2,1)}), bf16[8,128,256]{2,1,0:T(8,128)(2,1)S(1)}, u32[]{:S(2)}, u32[]{:S(2)}) async-start(bf16[8,128,256]{2,1,0:T(8,128)(2,1)} %bitcast.15), calls=%async_computation.2 | async-start | bytes 1048576 | tf_op jit(solution)/shard_map/all_to_all | solution.py:345
  74.8 1.2 %copy-start.16 = (bf16[2048,256]{1,0:T(8,128)(2,1)S(1)}, bf16[2048,256]{1,0:T(8,128)(2,1)}, u32[]{:S(2)}) copy-start(bf16[2048,256]{1,0:T(8,128)(2,1)} %copy-done.15) | copy-start | bytes 3145732
  76.1 1.2 %copy-start.18 = (bf16[2048,256]{1,0:T(8,128)(2,1)S(1)}, bf16[2048,256]{1,0:T(8,128)(2,1)}, u32[]{:S(2)}) copy-start(bf16[2048,256]{1,0:T(8,128)(2,1)} %copy-done.17) | copy-start | bytes 3145732
  77.3 0.8 copy-start.20

commit v2 on v1

--- a/solution.py
+++ b/solution.py
@@ -29,7 +29,7 @@
     return high, low
 
 
-def call(kernel, outs, args, grid=None, in_specs=None, out_specs=None, scratch=(), flops=0, moved=0, trans=0, name=None, prefetch=0):
+def call(kernel, outs, args, grid=None, in_specs=None, out_specs=None, scratch=(), flops=0, moved=0, trans=0, name=None, prefetch=0, vmem=64):
     spec = pltpu.PrefetchScalarGridSpec(
         num_scalar_prefetch=prefetch,
         grid=grid or (1,),
@@ -42,7 +42,7 @@
         out_shape=outs,
         grid_spec=spec,
         name=name,
-        compiler_params=pltpu.CompilerParams(vmem_limit_bytes=48 << 20),
+        compiler_params=pltpu.CompilerParams(vmem_limit_bytes=min(vmem << 20, 67043328)),
         cost_estimate=pl.CostEstimate(flops=int(flops), bytes_accessed=int(moved), transcendentals=int(trans)),
     )(*args)
 

time: 109 us -> 107 us (0.982)
  local copies, waits for them, and re-layouts: 14.8 us -> 1.29 us
  Pallas kernels: 34.4 us -> 44.7 us
  starting transfers between devices: 18.3 us -> 20.1 us
    unnamed x44 -> x0, local copies, waits for them, and re-layouts: 14.8 us -> none
    pallas_call x6, Pallas kernels: 34.4 us -> 44.7 us  [call(): pl.pallas_call(kernel, out_shape=outs, grid_spec=spec, name=name, compile...]
    reshape x1, local copies, waits for them, and re-layouts: 0.01 us -> 1.29 us  [local(): gate_bias.reshape(1, -1)]
  transfers between devices with their start and end apart: 3 -> 3, of which waited for: 3 -> 3; matrix products, arithmetic and copies ran while one was open for 0% -> 1% of each run, Pallas kernels for 11% -> 15%
where the time goes in v2:
time: 107 us
  Pallas kernels  44.7 us (42%)
  blocking collectives  20.4 us (19%)
  starting transfers between devices  20.1 us (19%)
  waiting for transfers between devices  19.3 us (18%)
  local copies, waits for them, and re-layouts  1.29 us (1%)
    pallas_call x6, Pallas kernels, call(): pl.pallas_call(kernel, out_shape=outs, grid_spec=spec, name=name, compile...  44.7 us
    all_to_all x1, blocking collectives, local(): lax.all_to_all(total.reshape(peers, group_rows // peers, width), 'event',...  20.4 us
    all_to_all x1, waiting for transfers between devices, local(): message = lax.all_to_all(message, ('node', 'event'), 0, 0, tiled=True)  15.9 us
    all_to_all x1, starting transfers between devices, local(): message = lax.all_to_all(message, ('node', 'event'), 0, 0, tiled=True)  11.6 us
    all_to_all x1, starting transfers between devices, local(): lax.all_to_all(table_grad.reshape(groups, per_group, width), 'node', 0, 0...  4.33 us
    all_to_all x1, starting transfers between devices, local(): lax.all_to_all(fetched.reshape(groups, per_group, width), 'node', 0, 0, t...  4.15 us
    all_to_all x1, waiting for transfers between devices, local(): lax.all_to_all(table_grad.reshape(groups, per_group, width), 'node', 0, 0...  3 us
  transfers between devices with their start and end apart: 3, of which 3 were waited for; matrix products, arithmetic and copies ran while one was open for 1% of the time, Pallas kernels for 15%

profile of v2, /device:TPU:0, one launch (start us, length us, event | category | flops | bytes accessed | tf_op | source)
XLA Modules:
  0.0 106.7 jit_solution(13629627698529183795)
XLA Ops:
  0.0 2.2 %pack.1 = bf16[128,24,128]{2,1,0:T(8,128)(2,1)} custom-call(bf16[128,16,128]{2,1,0:T(8,128)(2,1)} %bitcast.23, s32[16,128]{1,0:T(8,128)} %bitcast.26, s32[16,128]{1,0:T(8,128)} %bitcast.27, s32[16,128]{1,0:T(8,128)} %bitcast.28, s32[16,128]{1,0:T(8,128)} %bitcast.29, s32[1,128]{1,0:T(1,128)} %count.1, s32[8,128]{1,0:T(8,128)} %bitcast.30), custom_call_target="tpu_custom_call" | custom-call | bytes 1048576 | tf_op jit(solution)/shard_map/pack/pallas_call | solution.py:40
  2.2 11.6 %all-to-all-start = ((bf16[128,24,128]{2,1,0:T(8,128)(2,1)}), bf16[128,24,128]{2,1,0:T(8,128)(2,1)}, u32[]{:S(2)}, u32[]{:S(2)}) async-start(bf16[128,24,128]{2,1,0:T(8,128)(2,1)} %pack.1), calls=%async_computation | async-start | bytes 1572864 | tf_op jit(solution)/shard_map/all_to_all | solution.py:271
  13.8 15.9 %all-to-all-done.tail.message = bf16[128,24,128]{2,1,0:T(8,128)(2,1)} async-done(((bf16[128,24,128]{2,1,0:T(8,128)(2,1)}), bf16[128,24,128]{2,1,0:T(8,128)(2,1)}, u32[]{:S(2)}, u32[]{:S(2)}) %all-to-all-start) | async-done | bytes 786464 | tf_op jit(solution)/shard_map/all_to_all | solution.py:271
  29.8 3.7 %fetch.1 = bf16[1024,256]{1,0:T(8,128)(2,1)} custom-call(s32[1]{0:T(128)} %bitcast.place, bf16[8,16,24,128]{3,2,1,0:T(8,128)(2,1)} %bitcast.11.tail, bf16[2048,256]{1,0:T(8,128)(2,1)} %memory.3), custom_call_target="tpu_custom_call" | custom-call | flops 1073741824 | bytes 1048576 | tf_op jit(solution)/shard_map/fetch/pallas_call | solution.py:40
  33.4 4.1 %all-to-all-start.1 = ((bf16[8,128,256]{2,1,0:T(8,128)(2,1)}), bf16[8,128,256]{2,1,0:T(8,128)(2,1)}, u32[]{:S(2)}, u32[]{:S(2)}) async-start(bf16[8,128,256]{2,1,0:T(8,128)(2,1)} %bitcast.25), calls=%async_computation.1 | async-start | bytes 1048576 | tf_op jit(solution)/shard_map/all_to_all | solution.py:286
  37.6 1.3 %reshape.32.bias = f32[1,768]{1,0:T(1,128)} reshape(f32[768]{0:T(1024)} %param.24) | data formatting | bytes 6144 | tf_op jit(solution)/shard_map/reshape | solution.py:322
  38.9 8.6 %source.1 = (bf16[2048,256]{1,0:T(8,128)(2,1)}, bf16[2048,128]{1,0:T(8,128)(2,1)}, f32[8,2048]{1,0:T(8,128)}) custom-call(bf16[128,24,128]{2,1,0:T(8,128)(2,1)} %all-to-all-done.tail.message, bf16[2048,256]{1,0:T(8,128)(2,1)} %memory.3, f32[1,128]{1,0:T(1,128)} %bitcast.31), custom_call_target="tpu_custom_call" | custom-call | flops 2147483648 | bytes 2097152 | tf_op jit(solution)/shard_map/source/pallas_call | solution.py:40
  47.5 0.4 all-to-all-done.1
  47.9 18.3 %step.1 = (bf16[1024,256]{1,0:T(8,128)(2,1)}, bf16[2048,256]{1,0:T(8,128)(2,1)}, bf16[2048,256]{1,0:T(8,128)(2,1)}) custom-call(bf16[128,24,128]{2,1,0:T(8,128)(2,1)} %all-to-all-done.tail.message, bf16[1024,256]{1,0:T(8,128)(2,1)} %bitcast.13.table, bf16[2048,256]{1,0:T(8,128)(2,1)} %get-tuple-element.11.current_ref, ...), custom_call_target="tpu_custom_call" | custom-call | flops 11005853696 | bytes 4194304 | tf_op jit(solution)/shard_map/step/pallas_call | solution.py:40
  66.1 4.3 %all-to-all-start.2 = ((bf16[8,128,256]{2,1,0:T(8,128)(2,1)}), bf16[8,128,256]{2,1,0:T(8,128)(2,1)}, u32[]{:S(2)}, u32[]{:S(2)}) async-start(bf16[8,128,256]{2,1,0:T(8,128)(2,1)} %bitcast.24), calls=%async_computation.2 | async-start | bytes 1048576 | tf_op jit(solution)/shard_map/all_to_all | solution.py:345
  70.5 7.4 %scatter.1.state_grad = f32[2048,256]{1,0:T(8,128)} custom-call(f32[8,2048]{1,0:T(8,128)} %get-tuple-element.14.rows, bf16[2048,256]{1,0:T(8,128)(2,1)} %get-tuple-element.15.grad_high, bf16[2048,256]{1,0:T(8,128)(2,1)} %get-tuple-element.16.grad_low), custom_call_target="tpu_custom_call" | custom-call | flops 4294967296 | bytes 4194304 | tf_op jit(solution)/shard_map/scatter/pallas_call | solution.py:40
  77.9 3.0 %all-to-all-done.2 = bf16[8,128,256]{2,1,0:T(8,128)(2,1)} async-done(((bf16[8,128,256]{2,1,0:T(8,128)(2,1)}), bf16[8,128,256]{2,1,0:T(8,128)(2,1)}, u32[]{:S(2)}, u32[]{:S(2)}) %all-to-all-start.2) | async-done | bytes 524320 | tf_op jit(solution)/shard_map/all_to_all | solution.py:345
  80.9 4.6 %returned.1 = bf16[2048,256]{1,0:T(8,128)(2,1)} custom-call(s32[1]{0:T(128)} %bitcast.place, bf16[8,16,24,128]{3,2,1,0:T(8,128)(2,1)} %bitcast.11.tail, bf16[1024,256]{1,0:T(8,128)(2,1)} %bitcast.16.returned, f32[2048,256]{1,0:T(8,128)} %scatter.1.state_grad), custom_call_target="tpu_custom_call" | custom-call | flops 1073741824 | bytes 3145728 | tf_op jit(solution)/shard_map/returned/pallas_call | solution.py:40
  85.5 20.4 %all_to_all.20 = bf16[16,128,256]{2,1,0:T(8,128)(2,1)S(1)} all-to-all(bf16[16,128,256]{2,1,0:T(8,128)(2,1)} %bitcast.22), channel_id=1, replica_groups=mesh['node'=8,'event'=16] {'event'}, dimensions={0} | all-to-all | bytes 2097152 | tf_op jit(solution)/shard_map/all_to_all | solution.py:374
  105.9 0.8 convert_reduce_fusion
Async XLA Ops:
  2.2 27.6 %all-to-all-start = ((bf16[128,24,128]{2,1,0:T(8,128)(2,1)}), bf16[128,24,128]{2,1,0:T(8,128)(2,1)}, u32[]{:S(2)}, u32[]{:S(2)}) async-start(bf16[128,24,128]{2,1,0:T(8,128)(2,1)} %pack.1), calls=%async_computation | async-start | bytes 1572864 | tf_op jit(solution)/shard_map/all_to_all | solution.py:271
  33.4 14.5 %all-to-all-start.1 = ((bf16[8,128,256]{2,1,0:T(8,128)(2,1)}), bf16[8,128,256]{2,1,0:T(8,128)(2,1)}, u32[]{:S(2)}, u32[]{:S(2)}) async-start(bf16[8,128,256]{2,1,0:T(8,128)(2,1)} %bitcast.25), calls=%async_computation.1 | async-start | bytes 1048576 | tf_op jit(solution)/shard_map/all_to_all | solution.py:286
  66.1 14.8 %all-to-all-start.2 = ((bf16[8,128,256]{2,1,0:T(8,128)(2,1)}), bf16[8,128,256]{2,1,0:T(8,128)(2,1)}, u32[]{:S(2)}, u32[]{:S(2)}) async-start(bf16[8,128,256]{2,1,0:T(8,128)(2,1)} %bitcast.24), calls=%async_computation.2 | async-start | bytes 1048576 | tf_op jit(solution)/shard_map/all_to_all | solution.py:345
